TPU v7x, 512 devices: a whole 4x4x16 slice. The times are simulated.
512 devices in a mesh: req: 128 (over x, z, core), tp: 4 (over y).
Axes of the slice: x: 4, y: 4, z: 16, core: 2. Of those that a mesh axis runs over, the one named last changes fastest.
Arguments:
- x_pre: bfloat16 [65536, 1280], P('req', 'tp'), may hold values from -6 to 6
- x_dec: bfloat16 [512, 1280], P('req', 'tp'), may hold values from -6 to 6
- norm_gain: float32 [1280], replicated, may hold values from 0.1 to 1.9
- w_qkv: bfloat16 [3, 1280, 1280], P(None, None, 'tp'), may hold values from -0.15625 to 0.15625
- w_out: bfloat16 [1280, 1280], P('tp'), may hold values from -0.625 to 0.625
- pre_keys: bfloat16 [49152, 1280], P('req', 'tp'), may hold values from -70 to 70
- pre_values: bfloat16 [49152, 1280], P('req', 'tp'), may hold values from -6 to 6
- pre_lens: int32 [128], P('req'), may hold values from 0 to 384, as said below
- dec_keys: bfloat16 [81920, 1280], P('req', 'tp'), may hold values from -70 to 70
- dec_values: bfloat16 [81920, 1280], P('req', 'tp'), may hold values from -6 to 6
- dec_lens: int32 [512], replicated, may hold values from 1 to 41600, as said below
Outputs:
- pre_out: bfloat16 [65536, 1280], P('req', 'tp')
- dec_out: bfloat16 [512, 1280], P('req', 'tp')
Inputs may be any that keep to these rules, and one draw needn't show every extreme that they name: `pre_lens`: at least one prefill block has all 384 cached rows valid. `dec_lens`: the lengths sum to 61440; request 0 has exactly 41600 rows, every other request fewer.
All inputs are finite; a program needn't handle non-finite values.
Results may differ from a plain program's by a relative error of at most 0.012.
The roundings to bfloat16 on the way count: a program that leaves them out, or rounds other values in their place, can miss the bound.
Values may be sent and summed in bfloat16 or wider, within the bound.
No kernel may reach another device: no remote copies, remote signals or barrier semaphores. Data moves between devices by JAX's collectives and lax.ppermute only.
A program may use at most 64 MiB of HBM per device.

v0:
```python
import math
import jax
import jax.numpy as jnp
from jax import lax
from jax.sharding import PartitionSpec as P

HD = 80
EPSILON = 1e-06
MASKED_SCORE = -1e30


def normalize(tokens, norm_gain):
    tokens_f = tokens.astype(jnp.float32)
    mean_square = jnp.mean(tokens_f * tokens_f, axis=-1, keepdims=True)
    return (tokens_f * lax.rsqrt(mean_square + EPSILON) * norm_gain).astype(jnp.bfloat16)


def project(hidden, w_qkv):
    return tuple(
        (
            jnp.dot(hidden, w_qkv[matrix_index], preferred_element_type=jnp.float32).astype(
                jnp.bfloat16
            )
            for matrix_index in range(3)
        )
    )


def rounded(weights):
    held = lax.optimization_barrier(weights.astype(jnp.bfloat16))
    return held.astype(jnp.float32)


def prefill_attention(
    query_pre, key_pre, value_pre, pre_keys, pre_values, prefix, local_heads, score_scale
):
    rows_pre = query_pre.shape[0]
    cached = pre_keys.shape[0]
    keys_all = jnp.concatenate([pre_keys, key_pre], axis=0).reshape(-1, local_heads, HD)
    values_all = jnp.concatenate([pre_values, value_pre], axis=0).reshape(-1, local_heads, HD)
    scores = (
        jnp.einsum(
            "phd,rhd->hpr",
            query_pre.reshape(rows_pre, local_heads, HD),
            keys_all,
            preferred_element_type=jnp.float32,
        )
        * score_scale
    )
    column = jnp.arange(keys_all.shape[0], dtype=jnp.int32)[None, :]
    position = jnp.arange(rows_pre, dtype=jnp.int32)[:, None]
    allowed = jnp.where(column < cached, column < prefix, column - cached <= position)
    scores = jnp.where(allowed[None], scores, MASKED_SCORE)
    row_top = jnp.max(scores, axis=-1, keepdims=True)
    weights = jnp.where(allowed[None], jnp.exp(scores - row_top), 0.0)
    totals = jnp.transpose(jnp.sum(weights, axis=-1))
    mixed = (
        jnp.einsum(
            "hpr,rhd->phd",
            weights.astype(jnp.bfloat16),
            values_all,
            preferred_element_type=jnp.float32,
        )
        / totals[..., None]
    )
    return mixed.reshape(rows_pre, local_heads * HD).astype(jnp.bfloat16)


def body(
    x_pre,
    x_dec,
    norm_gain,
    w_qkv,
    w_out,
    pre_keys,
    pre_values,
    pre_lens,
    dec_keys,
    dec_values,
    dec_lens,
):
    full_pre, full_dec = (
        lax.all_gather(x_pre, "tp", axis=1, tiled=True),
        lax.all_gather(x_dec, "tp", axis=1, tiled=True),
    )
    local_width = w_qkv.shape[2]
    local_heads = local_width // HD
    score_scale = 1.0 / math.sqrt(HD)
    query_pre, key_pre, value_pre = project(normalize(full_pre, norm_gain), w_qkv)
    query_dec, key_dec, value_dec = project(normalize(full_dec, norm_gain), w_qkv)
    attn_pre = prefill_attention(
        query_pre, key_pre, value_pre, pre_keys, pre_values, pre_lens[0], local_heads, score_scale
    )
    all_queries = lax.all_gather(query_dec, "req", axis=0, tiled=True)
    requests = all_queries.shape[0]
    own_rows = query_dec.shape[0]
    pool_rows = dec_keys.shape[0]
    device = lax.axis_index("req")
    starts = jnp.cumsum(dec_lens) - dec_lens
    global_rows = device * pool_rows + jnp.arange(pool_rows, dtype=jnp.int32)
    allowed = (global_rows[None, :] >= starts[:, None]) & (
        global_rows[None, :] < (starts + dec_lens)[:, None]
    )
    cache_scores = (
        jnp.einsum(
            "qhd,rhd->qhr",
            all_queries.reshape(requests, local_heads, HD),
            dec_keys.reshape(pool_rows, local_heads, HD),
            preferred_element_type=jnp.float32,
        )
        * score_scale
    )
    cache_scores = jnp.where(allowed[:, None, :], cache_scores, MASKED_SCORE)
    self_score = (
        jnp.sum(
            query_dec.astype(jnp.float32).reshape(own_rows, local_heads, HD)
            * key_dec.astype(jnp.float32).reshape(own_rows, local_heads, HD),
            axis=-1,
        )
        * score_scale
    )
    self_rows = lax.dynamic_update_slice_in_dim(
        jnp.full((requests, local_heads), MASKED_SCORE, jnp.float32),
        self_score,
        device * own_rows,
        0,
    )
    local_top = jnp.maximum(jnp.max(cache_scores, axis=-1), self_rows)
    row_top = lax.pmax(local_top, "req")
    weights = jnp.where(allowed[:, None, :], jnp.exp(cache_scores - row_top[..., None]), 0.0)
    totals = jnp.sum(weights, axis=-1)
    partial_value = jnp.einsum(
        "qhr,rhd->qhd",
        weights.astype(jnp.bfloat16),
        dec_values.reshape(pool_rows, local_heads, HD),
        preferred_element_type=jnp.float32,
    ).reshape(requests, local_width)
    totals_all, partial_all = lax.psum((totals, partial_value), "req")
    own_totals = lax.dynamic_slice_in_dim(totals_all, device * own_rows, own_rows, 0)
    own_partial = lax.dynamic_slice_in_dim(partial_all, device * own_rows, own_rows, 0)
    own_top = lax.dynamic_slice_in_dim(row_top, device * own_rows, own_rows, 0)
    self_weight = jnp.exp(self_score - own_top)
    numerator = own_partial.reshape(own_rows, local_heads, HD) + rounded(self_weight)[
        ..., None
    ] * value_dec.astype(jnp.float32).reshape(own_rows, local_heads, HD)
    denominator = own_totals + self_weight
    attn_dec = (
        (numerator / denominator[..., None]).reshape(own_rows, local_width).astype(jnp.bfloat16)
    )
    terms_pre = jnp.dot(attn_pre, w_out, preferred_element_type=jnp.float32)
    terms_dec = jnp.dot(attn_dec, w_out, preferred_element_type=jnp.float32)
    out_pre, out_dec = (
        lax.psum_scatter(terms_pre, "tp", scatter_dimension=1, tiled=True),
        lax.psum_scatter(terms_dec, "tp", scatter_dimension=1, tiled=True),
    )
    return (out_pre.astype(jnp.bfloat16), out_dec.astype(jnp.bfloat16))


def solution(mesh):
    return jax.shard_map(
        body,
        mesh=mesh,
        in_specs=(
            P("req", "tp"),
            P("req", "tp"),
            P(),
            P(None, None, "tp"),
            P("tp", None),
            P("req", "tp"),
            P("req", "tp"),
            P("req"),
            P("req", "tp"),
            P("req", "tp"),
            P(),
        ),
        out_specs=(P("req", "tp"), P("req", "tp")),
        check_vma=False,
    )
```

profile of v0, /device:TPU:1, one launch (start us, length us, event | category | flops | bytes accessed | tf_op | source)
XLA Modules:
  0.0 785.2 jit_solution(5157148201678637434)
XLA Ops:
  8.1 10.6 %all-gather = bf16[4,320,4]{1,2,0:T(4,128)(2,1)S(1)} all-gather(bf16[1,320,4]{1,2,0:T(4,128)(2,1)} %bitcast.80), channel_id=1, replica_groups=mesh['req'=128,'tp'=4] {'tp'}, dimensions={0}, use_global_device_ids=true | all-gather | bytes 12800 | tf_op jit(solution)/shard_map/all_gather | solution.py:84
  18.9 0.8 multiply_convert_fusion
  19.7 1.4 convolution_convert_fusion.5
  21.1 1.5 fusion.36
  22.9 1.0 reduce-window.9
  24.1 0.8 fusion.64
  24.9 92.8 %all-gather.1 = bf16[128,4,320]{2,1,0:T(4,128)(2,1)S(1)} all-gather(bf16[1,4,320]{2,1,0:T(4,128)(2,1)S(1)} %bitcast.78), channel_id=1, replica_groups=mesh['req'=128,'tp'=4] {'req'}, dimensions={0}, use_global_device_ids=true | all-gather | bytes 330240 | tf_op jit(solution)/shard_map/all_gather | solution.py:94
  117.7 0.4 reshape.203
  118.4 0.3 compare_and_fusion
  118.7 3.6 bitcast_reduce_fusion
  122.3 250.3 %pmax.7 = f32[512,4]{0,1:T(4,128)S(1)} all-reduce(f32[512,4]{0,1:T(4,128)S(1)} %max.5), channel_id=1, replica_groups=mesh['req'=128,'tp'=4] {'req'}, use_global_device_ids=true, to_apply=%region_9.10 | all-reduce | flops 2048 | bytes 16384 | tf_op jit(solution)/shard_map/pmax | solution.py:129
  372.6 3.6 fusion.16
  376.2 1.1 copy.23
  377.5 0.5 all-gather.4.cloned.1.call-update
  378.0 3.8 fusion.6
  381.9 253.8 %psum.15 = f32[512,4]{0,1:T(4,128)S(1)} all-reduce(f32[512,4]{0,1:T(4,128)S(1)} %fusion.6), channel_id=1, replica_groups=mesh['req'=128,'tp'=4] {'req'}, use_global_device_ids=true, to_apply=%region_12.13 | all-reduce | flops 2048 | bytes 16384 | tf_op jit(solution)/shard_map/psum | solution.py:138
  636.9 1.1 fusion.20
  638.1 63.4 %all-reduce.2.cloned.1.call-done = f32[512,320]{1,0:T(8,128)} async-done(((f32[512,320]{1,0:T(8,128)}), f32[512,320]{1,0:T(8,128)}) %all-reduce.2.cloned.1.call-update) | async-done | bytes 655376 | tf_op jit(solution)/shard_map/psum | solution.py:138
  701.5 2.9 convolution_bitcast_fusion
  704.7 1.7 fusion.13
  706.4 2.1 convolution_convert_fusion
  708.5 0.9 pad_maximum_fusion.1
  709.4 0.7 convolution_convert_fusion.2
  710.1 0.9 pad_maximum_fusion
  710.9 1.4 convolution_convert_fusion.1
  712.4 6.7 fusion.65
  719.1 3.3 fusion.27
  722.4 2.4 fusion.66
  724.8 5.1 reduce-scatter.7.cloned.1.call-done
  729.9 1.6 copy.27
  731.5 44.2 %reduce-scatter.5.cloned.1.call-done = f32[512,320]{0,1:T(8,128)} async-done(((f32[512,1280]{0,1:T(8,128)}), f32[512,320]{0,1:T(8,128)}) %reduce-scatter.5.cloned.1.call-update) | async-done | bytes 655376 | tf_op jit(solution)/shard_map/reduce_scatter | solution.py:153
  775.7 1.9 convert_element_type.74
  (51 shorter events, 2.1 us)
Async XLA Ops:
  8.0 693.5 %copy-start = (bf16[320,1280]{1,0:T(8,128)(2,1)S(1)}, bf16[320,1280]{1,0:T(8,128)(2,1)}, u32[]{:S(2)}) copy-start(bf16[320,1280]{1,0:T(8,128)(2,1)} %param.15) | copy-start | bytes 2457604
  8.0 110.7 %copy-start.7 = (bf16[640,320]{0,1:T(8,128)(2,1)S(1)}, bf16[640,320]{0,1:T(8,128)(2,1)}, u32[]{:S(2)}) copy-start(bf16[640,320]{0,1:T(8,128)(2,1)} %param.19) | copy-start | bytes 1228804
  8.0 693.5 %all-reduce.2.cloned.1.call-start = ((), (), s32[]{:S(2)}) async-start(), calls=%async_computation.4 | async-start | bytes 1572864 | tf_op jit(solution)/shard_map/psum | solution.py:138
  118.7 253.9 %copy-start.8 = (bf16[640,320]{0,1:T(8,128)(2,1)S(1)}, bf16[640,320]{0,1:T(8,128)(2,1)}, u32[]{:S(2)}) copy-start(bf16[640,320]{0,1:T(8,128)(2,1)} %param.20) | copy-start | bytes 1228804
  377.4 327.3 %all-gather.4.cloned.1.call-start = ((), (), s32[]{:S(2)}) async-start(), calls=%async_computation.2 | async-start | bytes 1638400 | tf_op jit(solution)/shard_map/all_gather | solution.py:83
  378.0 351.9 %reduce-scatter.7.cloned.1.call-start = ((), (), s32[]{:S(2)}) async-start(), calls=%async_computation.5 | async-start | bytes 819200
  381.8 324.6 %copy-start.1 = (bf16[3,1280,320]{1,2,0:T(8,128)(2,1)S(1)}, bf16[3,1280,320]{1,2,0:T(8,128)(2,1)}, u32[]{:S(2)}) copy-start(bf16[3,1280,320]{1,2,0:T(8,128)(2,1)} %param.14) | copy-start | bytes 7372804
  381.8 324.5 %copy-start.6 = (f32[1280]{0:T(1024)S(1)}, f32[1280]{0:T(1024)}, u32[]{:S(2)}) copy-start(f32[1280]{0:T(1024)} %param.13) | copy-start | bytes 15364
  704.5 4.1 copy-start.4
  704.5 71.2 %reduce-scatter.5.cloned.1.call-start = ((), (), s32[]{:S(2)}) async-start(), calls=%async_computation.3 | async-start | bytes 3276800 | tf_op jit(solution)/shard_map/reduce_scatter | solution.py:153
  706.4 3.0 copy-start.2
  708.5 1.6 copy-start.5
  712.4 6.7 copy-start.3
Sparse Core Ops, SparseCore 0:
  377.5 323.8 all-reduce.1
Sparse Core Ops, SparseCore 1:
  380.0 21.8 all-gather.3
  704.5 25.3 reduce-scatter.6
  732.6 43.1 reduce-scatter.4
where the time goes:
time: 786 us; the launch traced here: 785 us
  blocking collectives  607 us (77%)
  waiting for transfers between devices  113 us (14%)
  matrix products  29.6 us (4%)
  between operations  16.5 us (2%)
  other arithmetic  13.4 us (2%)
    psum x1, blocking collectives, body(): totals_all, partial_all = lax.psum((totals, partial_value), 'req')  254 us
    pmax x1, blocking collectives, body(): row_top = lax.pmax(local_top, 'req')  250 us
    all_gather x1, blocking collectives, body(): all_queries = lax.all_gather(query_dec, 'req', axis=0, tiled=True)  92.8 us
    psum x1, waiting for transfers between devices, body(): totals_all, partial_all = lax.psum((totals, partial_value), 'req')  63.4 us
    reduce_scatter x1, waiting for transfers between devices, body(): lax.psum_scatter(terms_pre, 'tp', scatter_dimension=1, tiled=True)  44.2 us
  transfers between devices with their start and end apart: 4, of which 3 were waited for; matrix products, arithmetic and copies ran while one was open for 4% of the time, Pallas kernels for 0%

commit v1 on v0

--- a/solution.py
+++ b/solution.py
@@ -7,6 +7,13 @@
 HD = 80
 EPSILON = 1e-06
 MASKED_SCORE = -1e30
+
+
+def exchange_gather(x, mesh_axis, along):
+    n_dev = lax.axis_size(mesh_axis)
+    tiles = jnp.stack([x for _ in range(n_dev)])
+    tiles = lax.all_to_all(tiles, mesh_axis, split_axis=0, concat_axis=0)
+    return jnp.concatenate(tiles, axis=along)
 
 
 def normalize(tokens, norm_gain):
@@ -91,7 +98,7 @@
     attn_pre = prefill_attention(
         query_pre, key_pre, value_pre, pre_keys, pre_values, pre_lens[0], local_heads, score_scale
     )
-    all_queries = lax.all_gather(query_dec, "req", axis=0, tiled=True)
+    all_queries = exchange_gather(query_dec, "req", 0)
     requests = all_queries.shape[0]
     own_rows = query_dec.shape[0]
     pool_rows = dec_keys.shape[0]

time: 786 us -> 739 us (0.940)
  blocking collectives: 607 us -> 514 us
  waiting for transfers between devices: 113 us -> 138 us
  starting transfers between devices: 0.35 us -> 22.8 us
    all_gather x1 -> x0, blocking collectives: 92.8 us -> none  [body(): all_queries = lax.all_gather(query_dec, 'req', axis=0, tiled=True)]
    all_to_all x0 -> x1, waiting for transfers between devices: none -> 24.8 us  [exchange_gather(): tiles = lax.all_to_all(tiles, mesh_axis, split_axis=0, concat_axis=0)]
    all_to_all x0 -> x1, starting transfers between devices: none -> 22.5 us  [exchange_gather(): tiles = lax.all_to_all(tiles, mesh_axis, split_axis=0, concat_axis=0)]
  transfers between devices with their start and end apart: 4 -> 5, of which waited for: 3 -> 4; matrix products, arithmetic and copies ran while one was open for 4% -> 4% of each run, Pallas kernels for 0% -> 0%
where the time goes in v1:
time: 739 us
  blocking collectives  514 us (70%)
  waiting for transfers between devices  138 us (19%)
  matrix products  29.6 us (4%)
  starting transfers between devices  22.8 us (3%)
  between operations  16.5 us (2%)
  other arithmetic  12.1 us (2%)
    pmax x1, blocking collectives, body(): row_top = lax.pmax(local_top, 'req')  252 us
    psum x1, blocking collectives, body(): totals_all, partial_all = lax.psum((totals, partial_value), 'req')  251 us
    psum x1, waiting for transfers between devices, body(): totals_all, partial_all = lax.psum((totals, partial_value), 'req')  63.5 us
    reduce_scatter x1, waiting for transfers between devices, body(): lax.psum_scatter(terms_pre, 'tp', scatter_dimension=1, tiled=True)  44.2 us
    all_to_all x1, waiting for transfers between devices, exchange_gather(): tiles = lax.all_to_all(tiles, mesh_axis, split_axis=0, concat_axis=0)  24.8 us
    all_to_all x1, starting transfers between devices, exchange_gather(): tiles = lax.all_to_all(tiles, mesh_axis, split_axis=0, concat_axis=0)  22.5 us
  transfers between devices with their start and end apart: 5, of which 4 were waited for; matrix products, arithmetic and copies ran while one was open for 4% of the time, Pallas kernels for 0%

profile of v1, /device:TPU:1, one launch (start us, length us, event | category | flops | bytes accessed | tf_op | source)
XLA Modules:
  0.0 738.6 jit_solution(16928343992734676572)
XLA Ops:
  8.0 10.6 %all-gather = bf16[4,320,4]{1,2,0:T(4,128)(2,1)S(1)} all-gather(bf16[1,320,4]{1,2,0:T(4,128)(2,1)} %bitcast.78), channel_id=1, replica_groups=mesh['req'=128,'tp'=4] {'tp'}, dimensions={0}, use_global_device_ids=true | all-gather | bytes 12800 | tf_op jit(solution)/shard_map/all_gather | solution.py:91
  18.8 0.8 multiply_convert_fusion
  19.6 1.4 convolution_convert_fusion.5
  21.1 0.9 stack.2
  21.9 22.5 %all-to-all-start = ((bf16[128,4,320]{2,1,0:T(4,128)(2,1)}), bf16[128,4,320]{2,1,0:T(4,128)(2,1)S(1)}, u32[]{:S(2)}, u32[]{:S(2)}) async-start(bf16[128,4,320]{2,1,0:T(4,128)(2,1)} %stack.2), calls=%async_computation.1 | async-start | bytes 786432 | tf_op jit(solution)/shard_map/all_to_all | solution.py:15
  44.5 1.4 fusion.36
  47.1 0.3 compare_and_fusion
  47.5 24.8 %all-to-all-done = bf16[128,4,320]{2,1,0:T(4,128)(2,1)S(1)} async-done(((bf16[128,4,320]{2,1,0:T(4,128)(2,1)}), bf16[128,4,320]{2,1,0:T(4,128)(2,1)S(1)}, u32[]{:S(2)}, u32[]{:S(2)}) %all-to-all-start) | async-done | bytes 327712 | tf_op jit(solution)/shard_map/all_to_all | solution.py:15
  72.3 0.4 reshape_reshape.3
  72.7 3.6 bitcast_reduce_fusion
  76.3 252.2 %pmax.7 = f32[512,4]{0,1:T(4,128)S(1)} all-reduce(f32[512,4]{0,1:T(4,128)S(1)} %max.5), channel_id=1, replica_groups=mesh['req'=128,'tp'=4] {'req'}, use_global_device_ids=true, to_apply=%region_9.10 | all-reduce | flops 2048 | bytes 16384 | tf_op jit(solution)/shard_map/pmax | solution.py:136
  328.5 3.6 fusion.16
  332.2 1.1 copy.23
  333.4 0.5 all-gather.3.cloned.1.call-update
  334.6 1.1 fusion.20
  335.8 3.8 fusion.6
  339.6 251.2 %psum.15 = f32[512,4]{0,1:T(4,128)S(1)} all-reduce(f32[512,4]{0,1:T(4,128)S(1)} %fusion.6), channel_id=1, replica_groups=mesh['req'=128,'tp'=4] {'req'}, use_global_device_ids=true, to_apply=%region_12.13 | all-reduce | flops 2048 | bytes 16384 | tf_op jit(solution)/shard_map/psum | solution.py:145
  591.4 63.5 %all-reduce.2.cloned.1.call-done = f32[512,320]{1,0:T(8,128)} async-done(((f32[512,320]{1,0:T(8,128)}), f32[512,320]{1,0:T(8,128)}) %all-reduce.2.cloned.1.call-update) | async-done | bytes 655376 | tf_op jit(solution)/shard_map/psum | solution.py:145
  654.9 2.9 convolution_bitcast_fusion
  658.1 1.7 fusion.13
  659.8 2.1 convolution_convert_fusion
  661.9 0.9 pad_maximum_fusion.1
  662.8 0.7 convolution_convert_fusion.2
  663.5 0.9 pad_maximum_fusion
  664.4 1.4 convolution_convert_fusion.1
  665.8 6.7 fusion.65
  672.5 3.3 fusion.27
  675.8 2.4 fusion.66
  678.2 5.1 reduce-scatter.7.cloned.1.call-done
  683.3 1.6 copy.27
  684.9 44.2 %reduce-scatter.5.cloned.1.call-done = f32[512,320]{0,1:T(8,128)} async-done(((f32[512,1280]{0,1:T(8,128)}), f32[512,320]{0,1:T(8,128)}) %reduce-scatter.5.cloned.1.call-update) | async-done | bytes 655376 | tf_op jit(solution)/shard_map/reduce_scatter | solution.py:160
  729.2 1.9 convert_element_type.74
  (55 shorter events, 2.5 us)
Async XLA Ops:
  8.0 646.9 %copy-start = (bf16[320,1280]{1,0:T(8,128)(2,1)S(1)}, bf16[320,1280]{1,0:T(8,128)(2,1)}, u32[]{:S(2)}) copy-start(bf16[320,1280]{1,0:T(8,128)(2,1)} %param.15) | copy-start | bytes 2457604
  8.0 38.2 %copy-start.7 = (s32[512]{0:T(512)S(1)}, s32[512]{0:T(512)}, u32[]{:S(2)}) copy-start(s32[512]{0:T(512)} %param.21) | copy-start | bytes 6148
  8.0 64.6 %copy-start.8 = (bf16[640,320]{0,1:T(8,128)(2,1)S(1)}, bf16[640,320]{0,1:T(8,128)(2,1)}, u32[]{:S(2)}) copy-start(bf16[640,320]{0,1:T(8,128)(2,1)} %param.19) | copy-start | bytes 1228804
  21.9 50.3 %all-to-all-start = ((bf16[128,4,320]{2,1,0:T(4,128)(2,1)}), bf16[128,4,320]{2,1,0:T(4,128)(2,1)S(1)}, u32[]{:S(2)}, u32[]{:S(2)}) async-start(bf16[128,4,320]{2,1,0:T(4,128)(2,1)} %stack.2), calls=%async_computation.1 | async-start | bytes 786432 | tf_op jit(solution)/shard_map/all_to_all | solution.py:15
  44.4 610.5 %all-reduce.2.cloned.1.call-start = ((), (), s32[]{:S(2)}) async-start(), calls=%async_computation.5 | async-start | bytes 1572864 | tf_op jit(solution)/shard_map/psum | solution.py:145
  72.7 255.8 %copy-start.9 = (bf16[640,320]{0,1:T(8,128)(2,1)S(1)}, bf16[640,320]{0,1:T(8,128)(2,1)}, u32[]{:S(2)}) copy-start(bf16[640,320]{0,1:T(8,128)(2,1)} %param.20) | copy-start | bytes 1228804
  333.3 324.8 %all-gather.3.cloned.1.call-start = ((), (), s32[]{:S(2)}) async-start(), calls=%async_computation.3 | async-start | bytes 1638400 | tf_op jit(solution)/shard_map/all_gather | solution.py:90
  333.9 349.4 %reduce-scatter.7.cloned.1.call-start = ((), (), s32[]{:S(2)}) async-start(), calls=%async_computation.6 | async-start | bytes 819200
  339.6 320.2 %copy-start.1 = (bf16[3,1280,320]{1,2,0:T(8,128)(2,1)S(1)}, bf16[3,1280,320]{1,2,0:T(8,128)(2,1)}, u32[]{:S(2)}) copy-start(bf16[3,1280,320]{1,2,0:T(8,128)(2,1)} %param.14) | copy-start | bytes 7372804
  339.6 320.2 %copy-start.6 = (f32[1280]{0:T(1024)S(1)}, f32[1280]{0:T(1024)}, u32[]{:S(2)}) copy-start(f32[1280]{0:T(1024)} %param.13) | copy-start | bytes 15364
  657.9 4.1 copy-start.4
  657.9 71.3 %reduce-scatter.5.cloned.1.call-start = ((), (), s32[]{:S(2)}) async-start(), calls=%async_computation.4 | async-start | bytes 3276800 | tf_op jit(solution)/shard_map/reduce_scatter | solution.py:160
  659.8 3.0 copy-start.2
  661.9 1.6 copy-start.5
  665.8 6.7 copy-start.3
Sparse Core Ops, SparseCore 0:
  333.5 321.4 all-reduce.1
Sparse Core Ops, SparseCore 1:
  335.9 19.2 all-gather.2
  658.0 25.3 reduce-scatter.6
  686.1 43.1 reduce-scatter.4
